TPU v7x, 128 devices: a whole 4x4x4 slice. The times are simulated.
128 devices in a mesh: batch: 8 (over y_lo, z), tensor: 16 (over y_hi, x, core).
Axes of the slice: x: 4, y: 4 (y_hi: 2, y_lo: 2; y = y_hi * 2 + y_lo), z: 4, core: 2. Of those that a mesh axis runs over, the one named last changes fastest.
Arguments:
- attn_values: bfloat16 [2048, 8192], P('batch', 'tensor'), may hold values from -6 to 6
- out_weight: bfloat16 [8192, 8192], P('tensor'), may hold values from -0.09375 to 0.09375
- residual_t: bfloat16 [8192, 2048], P('tensor', 'batch'), may hold values from -6 to 6
- projector: bfloat16 [8192, 4096], P('tensor'), may hold values from -0.0625 to 0.0625
- student_input: bfloat16 [2048, 4096], P('batch', 'tensor'), may hold values from -6 to 6
- norm_gain: float32 [4096], replicated, may hold values from 0.1 to 1.9
- w_gate: bfloat16 [4096, 8192], P('batch', 'tensor'), may hold values from -0.09375 to 0.09375
- w_up: bfloat16 [4096, 8192], P('batch', 'tensor'), may hold values from -0.09375 to 0.09375
- w_down: bfloat16 [4096, 8192], P('batch', 'tensor'), may hold values from -0.0625 to 0.0625
- route_index: int32 [8, 64], P('batch'), may hold values from -1 to 255, as said below
Outputs:
- teacher_hidden: bfloat16 [8192, 2048], P('tensor', 'batch')
- grad_gate: float32 [4096, 8192], P('batch', 'tensor')
- grad_up: float32 [4096, 8192], P('batch', 'tensor')
- grad_down: float32 [4096, 8192], P('batch', 'tensor')
Inputs may be any that keep to these rules, and one draw needn't show every extreme that they name: `route_index`: in each batch group the live slots come first, hold distinct positions in increasing order, and the empty slots after them hold -1. The batch groups hold 256 live slots together, and some batch group has all 64 slots live.
All inputs are finite; a program needn't handle non-finite values.
Results may differ from a plain program's by a relative error of at most 0.025.
Values may be sent and summed in bfloat16 or wider, within the bound.
No kernel may reach another device: no remote copies, remote signals or barrier semaphores. Data moves between devices by JAX's collectives and lax.ppermute only.
A program may use at most 128 MiB of HBM per device.

v0:
```python
import math
import jax
import jax.numpy as jnp
from jax import lax
from jax.sharding import Mesh
from jax.sharding import PartitionSpec as P

TENSOR = ("tensor_0", "tensor_1", "tensor_2")
epsilon = 1e-05


def from_everyone(value, axis):
    copies = jnp.broadcast_to(value, (lax.axis_size(axis), *value.shape))
    return lax.all_to_all(copies, axis, split_axis=0, concat_axis=0, tiled=True)


def joined_along(blocks, dim):
    lengths = list(blocks.shape[1:])
    lengths[dim] *= blocks.shape[0]
    return jnp.moveaxis(blocks, 0, dim).reshape(lengths)


def collect(value, axis, dim):
    blocks = from_everyone(value, axis)
    return joined_along(blocks, dim)


def side_by_side(arrays, axis, dim, along):
    ends, at = ([], 0)
    for a in arrays[:-1]:
        at += a.shape[along]
        ends.append(at)
    both = jnp.concatenate(arrays, axis=along)
    return tuple(jnp.split(lax.all_gather(both, axis, axis=dim, tiled=True), ends, axis=along))


def cut_along(value, dim, devices):
    lengths = value.shape
    blocks = value.reshape(*lengths[:dim], devices, lengths[dim] // devices, *lengths[dim + 1 :])
    return jnp.moveaxis(blocks, dim, 0)


def sent_and_summed(value, axis, dim):
    devices = lax.axis_size(axis)
    blocks = lax.all_to_all(cut_along(value, dim, devices), axis, 0, 0, tiled=True)
    return jnp.sum(blocks.astype(jnp.float32), axis=0)


def summed_rows(value, axes, dim):
    far, near = axes
    own = sent_and_summed(cut_along(value, dim, lax.axis_size(far)), near, dim + 1)
    return jnp.sum(
        lax.all_to_all(own.astype(jnp.bfloat16), far, 0, 0, tiled=True).astype(jnp.float32), axis=0
    )


def filled_up(lines, devices):
    spare = -len(lines) % devices
    return jnp.pad(lines, [(0, spare)] + [(0, 0)] * (lines.ndim - 1))


def gather_axes(value, axes, dim):
    far, near = axes
    blocks = from_everyone(from_everyone(value, far), near)
    return joined_along(blocks.swapaxes(0, 1).reshape(-1, *value.shape), dim)


def total_of(value, axes):
    lines = value.reshape(-1, value.shape[-1])
    own = summed_rows(filled_up(lines, lax.axis_size(axes[0]) * lax.axis_size(axes[1])), axes, 0)
    whole = gather_axes(own.astype(jnp.bfloat16), axes, 0)
    return whole[: len(lines)].reshape(value.shape).astype(jnp.float32)


def grouped_product(left, right):
    dims = (((1,), (1,)), ((0,), (0,)))
    full = lax.dot_general(left, right, dims, preferred_element_type=jnp.float32)
    rounded = lax.optimization_barrier(full.astype(jnp.bfloat16))
    return jnp.sum(rounded.astype(jnp.float32), axis=0)


def on_device(
    attn_values,
    out_weight,
    residual_t,
    projector,
    student_input,
    norm_gain,
    w_gate,
    w_up,
    w_down,
    route_index,
):
    summed = lax.psum_scatter(
        lax.dot_general(
            out_weight, attn_values, (((0,), (1,)), ((), ())), preferred_element_type=jnp.float32
        ).astype(jnp.bfloat16),
        TENSOR,
        scatter_dimension=0,
        tiled=True,
    ).astype(jnp.float32)
    teacher_hidden = (residual_t.astype(jnp.float32) + summed).astype(jnp.bfloat16)
    slot_pos = route_index[0]
    present = slot_pos >= 0
    safe_slot = jnp.maximum(slot_pos, 0)
    routed_teacher = jnp.where(present[None, :], jnp.take(teacher_hidden, safe_slot, axis=1), 0)
    target_part = lax.dot_general(
        routed_teacher, projector, (((0,), (0,)), ((), ())), preferred_element_type=jnp.float32
    )
    local_rows = jnp.where(present[:, None], jnp.take(student_input, safe_slot, axis=0), 0)
    routed_input = collect(local_rows, TENSOR, 1).astype(jnp.float32)
    mean_square = jnp.mean(routed_input * routed_input, axis=1, keepdims=True)
    normed = (routed_input * lax.rsqrt(mean_square + epsilon) * norm_gain[None, :]).astype(
        jnp.bfloat16
    )
    slot_total = normed.shape[0]
    local_units = w_gate.shape[1]
    gate_full, up_full, down_full = side_by_side((w_gate, w_up, w_down), "batch", 0, 1)
    gate_act = jnp.dot(normed, gate_full, preferred_element_type=jnp.float32)
    up_act = jnp.dot(normed, up_full, preferred_element_type=jnp.float32)
    sigma_gate = jax.nn.sigmoid(gate_act)
    hidden = (gate_act * sigma_gate * up_act).astype(jnp.bfloat16)
    out_part = lax.dot_general(
        hidden, down_full, (((1,), (1,)), ((), ())), preferred_element_type=jnp.float32
    )
    misfit = total_of(
        (out_part - target_part).astype(jnp.bfloat16), (("tensor_0", "tensor_1"), "tensor_2")
    )
    group_count = lax.axis_size("batch")
    mean_routed = student_input.shape[0] // 8
    loss_scale = 1.0 / math.sqrt(mean_routed * group_count)
    grad_out = (jnp.where(present[:, None], misfit, 0.0) * loss_scale).astype(jnp.bfloat16)
    grad_hidden = jnp.dot(grad_out, down_full, preferred_element_type=jnp.float32)
    grad_gate_act = (
        grad_hidden * up_act * sigma_gate * (1.0 + gate_act * (1.0 - sigma_gate))
    ).astype(jnp.bfloat16)
    grad_up_act = (grad_hidden * gate_act * sigma_gate).astype(jnp.bfloat16)
    rows_local = w_gate.shape[0]
    every_normed, every_grad = (
        lax.all_to_all(normed, "batch", split_axis=1, concat_axis=0, tiled=True),
        lax.all_to_all(grad_out, "batch", split_axis=1, concat_axis=0, tiled=True),
    )
    every_gate, every_up, every_hidden = side_by_side(
        (grad_gate_act, grad_up_act, hidden), "batch", 0, 1
    )
    normed_groups = every_normed.reshape(group_count, slot_total, rows_local)
    grad_groups = every_grad.reshape(group_count, slot_total, rows_local)
    gate_groups = every_gate.reshape(group_count, slot_total, local_units)
    up_groups = every_up.reshape(group_count, slot_total, local_units)
    hidden_groups = every_hidden.reshape(group_count, slot_total, local_units)
    grad_gate = grouped_product(normed_groups, gate_groups)
    grad_up = grouped_product(normed_groups, up_groups)
    grad_down = grouped_product(grad_groups, hidden_groups)
    return (teacher_hidden, grad_gate, grad_up, grad_down)


def solution(mesh):
    split = Mesh(
        mesh.devices.reshape(mesh.shape["batch"], 2, 4, 2),
        ("batch", "tensor_0", "tensor_1", "tensor_2"),
    )
    in_specs = (
        P("batch", TENSOR),
        P(TENSOR, None),
        P(TENSOR, "batch"),
        P(TENSOR, None),
        P("batch", TENSOR),
        P(),
        P("batch", TENSOR),
        P("batch", TENSOR),
        P("batch", TENSOR),
        P("batch", None),
    )
    out_specs = (P(TENSOR, "batch"), P("batch", TENSOR), P("batch", TENSOR), P("batch", TENSOR))
    return jax.shard_map(
        on_device, mesh=split, in_specs=in_specs, out_specs=out_specs, check_vma=False
    )
```

profile of v0, /device:TPU:18, one launch (start us, length us, event | category | flops | bytes accessed | tf_op | source)
XLA Modules:
  0.0 288.8 jit_solution(2432564171475395224)
XLA Ops:
  8.1 0.9 copy-done
  9.0 7.7 %convolution_convert_fusion = bf16[8192,256]{1,0:T(8,128)(2,1)} fusion(bf16[512,8192]{1,0:T(8,128)(2,1)} %param.11, bf16[256,512]{1,0:T(8,128)(2,1)S(1)} %copy-done), kind=kOutput, calls=%fused_computation.2 | convolution fusion | flops 2149580800 | bytes 12845056 | tf_op jit(solution)/shard_map/dot_general | solution.py:95
  16.8 0.9 copy-done.7
  18.0 1.3 pad_maximum_fusion
  20.3 14.8 %all_to_all.51 = bf16[16,64,256]{2,1,0:T(8,128)(2,1)S(1)} all-to-all(bf16[16,64,256]{2,1,0:T(8,128)(2,1)S(1)} %broadcast_in_dim.78), channel_id=1, replica_groups=mesh['batch'=8,'tensor_0'=2,'tensor_1'=4,'tensor_2'=2] {'tensor_0','tens..., dimensions={0} | all-to-all | bytes 1048576 | tf_op jit(solution)/shard_map/all_to_all | solution.py:14
  35.6 88.8 %reduce-scatter.2.cloned.1.call-done = bf16[512,256]{1,0:T(8,128)(2,1)} async-done(((bf16[8192,256]{1,0:T(8,128)(2,1)}), bf16[512,256]{1,0:T(8,128)(2,1)}) %reduce-scatter.2.cloned.1.call-update) | async-done | bytes 262160 | tf_op jit(solution)/shard_map/reduce_scatter | solution.py:94
  124.4 1.0 add_convert_fusion
  125.6 0.7 gather_fusion.1
  126.3 45.2 %all-gather.3.cloned.1.call-done = bf16[4096,1536]{1,0:T(8,128)(2,1)} async-done(((bf16[512,1536]{1,0:T(8,128)(2,1)}), bf16[4096,1536]{1,0:T(8,128)(2,1)}) %all-gather.3.cloned.1.call-update) | async-done | bytes 12582928 | tf_op jit(solution)/shard_map/all_gather | solution.py:34
  171.5 3.1 %fusion.3 = f32[64,512]{1,0:T(8,128)S(1)} fusion(bf16[4096,1536]{1,0:T(8,128)(2,1)} %all-gather.3.cloned.1.call-done, f32[64,4096]{1,0:T(8,128)S(1)} %bitcast.38, f32[4096]{0:T(1024)S(1)} %copy-done.11, f32[64]{0:T(128)S(1)} %add_rsqrt_fusion), kind=kOutput, calls=%fused_computation.10 | convolution fusion | flops 269221888 | bytes 5390592 | tf_op jit(solution)/shard_map/dot_general | solution.py:119
  174.6 3.7 %multiply_convert_fusion.5 = (bf16[64,512]{1,0:T(8,128)(2,1)S(1)}, f32[64,512]{1,0:T(8,128)}) fusion(f32[64,512]{1,0:T(8,128)S(1)} %fusion.3, bf16[4096,1536]{1,0:T(8,128)(2,1)} %all-gather.3.cloned.1.call-done, f32[64,4096]{1,0:T(8,128)S(1)} %bitcast.39, f32[4096]{0:T(1024)S(1)} %copy-done.11, f32[64]{0:T(128)S(1)} %add_rsqrt_fusion), kind=kOutput, calls=%fused_computation.44 | convolution fusion | flops 269418496 | bytes 5587200 | tf_op jit(solution)/shard_map/dot_general | solution.py:120
  178.3 3.7 %fusion.7 = f32[64,4096]{1,0:T(8,128)S(1)} fusion(bf16[64,512]{1,0:T(8,128)(2,1)S(1)} %get-tuple-element.13, bf16[4096,1536]{1,0:T(8,128)(2,1)} %all-gather.3.cloned.1.call-done), kind=kOutput, calls=%fused_computation.14 | convolution fusion | flops 268435456 | bytes 5308416 | tf_op jit(solution)/shard_map/dot_general | solution.py:123
  182.1 0.9 fusion
  183.4 4.2 %all_to_all.52 = bf16[2,8,4,4096]{3,2,1,0:T(4,128)(2,1)S(1)} all-to-all(bf16[2,8,4,4096]{3,2,1,0:T(4,128)(2,1)S(1)} %bitcast.37), channel_id=1, replica_groups=mesh['batch'=8,'tensor_0'=2,'tensor_1'=4,'tensor_2'=2] {'tensor_2'}, dimensions={0} | all-to-all | bytes 1048576 | tf_op jit(solution)/shard_map/all_to_all | solution.py:45
  188.0 12.5 %all_to_all.53 = bf16[8,4,4096]{2,1,0:T(4,128)(2,1)S(1)} all-to-all(bf16[8,4,4096]{2,1,0:T(4,128)(2,1)S(1)} %reduce_sum.61), channel_id=1, replica_groups=mesh['batch'=8,'tensor_0'=2,'tensor_1'=4,'tensor_2'=2] {'tensor_0','tens..., dimensions={0} | all-to-all | bytes 524288 | tf_op jit(solution)/shard_map/all_to_all | solution.py:53
  200.8 11.3 %all_to_all.54 = bf16[8,4,4096]{2,1,0:T(4,128)(2,1)S(1)} all-to-all(bf16[8,4,4096]{2,1,0:T(4,128)(2,1)S(1)} %broadcast_in_dim.84), channel_id=1, replica_groups=mesh['batch'=8,'tensor_0'=2,'tensor_1'=4,'tensor_2'=2] {'tensor_0','tens..., dimensions={0} | all-to-all | bytes 524288 | tf_op jit(solution)/shard_map/all_to_all | solution.py:14
  212.3 4.2 %all_to_all.55 = bf16[2,8,4,4096]{3,2,1,0:T(4,128)(2,1)S(1)} all-to-all(bf16[2,8,4,4096]{3,2,1,0:T(4,128)(2,1)S(1)} %broadcast_in_dim.85), channel_id=1, replica_groups=mesh['batch'=8,'tensor_0'=2,'tensor_1'=4,'tensor_2'=2] {'tensor_2'}, dimensions={0} | all-to-all | bytes 1048576 | tf_op jit(solution)/shard_map/all_to_all | solution.py:14
  217.0 3.1 %multiply_convert_fusion.4 = (bf16[64,512]{1,0:T(8,128)(2,1)S(1)}, bf16[64,512]{1,0:T(8,128)(2,1)S(1)}) fusion(f32[64,512]{1,0:T(8,128)S(1)} %fusion.3, f32[64,512]{1,0:T(8,128)} %get-tuple-element.14, bf16[4096,1536]{1,0:T(8,128)(2,1)} %all-gather.3.cloned.1.call-done, f32[64,4096]{1,0:T(8,128)S(1)} %reshape.96, pred[64]{0:T(512)(128)(4,1)S(1)} %get-tuple-element.11), kind=kOutput, calls=%fused_computation.43 | convolution fusion | flops 269647872 | bytes 5636160 | tf_op jit(solution)/shard_map/dot_general | solution.py:133
  221.8 1.4 fusion.13
  223.2 3.7 %all-to-all-start.1 = ((bf16[64,8,512]{2,0,1:T(8,128)(2,1)}), bf16[64,8,512]{2,0,1:T(8,128)(2,1)S(1)}, u32[]{:S(2)}, u32[]{:S(2)}) async-start(bf16[64,8,512]{2,0,1:T(8,128)(2,1)} %fusion.13), calls=%async_computation.2 | async-start | bytes 1048576 | tf_op jit(solution)/shard_map/all_to_all | solution.py:140
  226.8 0.7 reshape.97
  227.6 1.4 fusion.11
  229.0 32.2 %all-gather.5.cloned.1.call-done = bf16[512,1536]{1,0:T(8,128)(2,1)} async-done(((bf16[64,1536]{1,0:T(8,128)(2,1)}), bf16[512,1536]{1,0:T(8,128)(2,1)}) %all-gather.5.cloned.1.call-update) | async-done | bytes 1572880 | tf_op jit(solution)/shard_map/all_gather | solution.py:34
  261.2 1.5 fusion.30
  262.7 4.0 %all-to-all-start.6 = ((bf16[64,8,512]{2,0,1:T(8,128)(2,1)}), bf16[64,8,512]{2,0,1:T(8,128)(2,1)S(1)}, u32[]{:S(2)}, u32[]{:S(2)}) async-start(bf16[64,8,512]{2,0,1:T(8,128)(2,1)} %fusion.11), calls=%async_computation.7 | async-start | bytes 1048576 | tf_op jit(solution)/shard_map/all_to_all | solution.py:141
  266.7 3.2 %convolution_convert_fusion.2 = bf16[8,512,512]{2,1,0:T(8,128)(2,1)} fusion(bf16[8,64,512]{2,1,0:T(8,128)(2,1)S(1)} %bitcast.36, bf16[64,8,512]{2,0,1:T(8,128)(2,1)S(1)} %all-to-all-done.1), kind=kOutput, calls=%fused_computation.17 | convolution fusion | flops 270532608 | bytes 5242880 | tf_op jit(solution)/shard_map/dot_general | solution.py:77
  270.0 3.3 %convolution_convert_fusion.3 = bf16[8,512,512]{2,1,0:T(8,128)(2,1)} fusion(bf16[8,64,512]{2,1,0:T(8,128)(2,1)S(1)} %bitcast.35, bf16[64,8,512]{2,0,1:T(8,128)(2,1)S(1)} %all-to-all-done.1), kind=kOutput, calls=%fused_computation.18 | convolution fusion | flops 270532608 | bytes 5242880 | tf_op jit(solution)/shard_map/dot_general | solution.py:77
  273.2 1.8 all-to-all-done.6
  275.0 1.3 convolution_convert_fusion.1
  276.3 1.6 convert_reduce_fusion
  277.9 0.9 copy-done.3
  278.9 2.5 convert_reduce_fusion.1
  (54 shorter events, 5.5 us)
Async XLA Ops:
  8.0 1.0 copy-start
  8.0 116.4 %reduce-scatter.2.cloned.1.call-start = ((), (), s32[]{:S(2)}) async-start(), calls=%async_computation.8 | async-start | bytes 4456448 | tf_op jit(solution)/shard_map/reduce_scatter | solution.py:94
  16.7 1.0 copy-start.7
  16.7 1.2 copy-start.8
  16.7 1.4 copy-start.9
  16.7 2.7 copy-start.12
  16.7 2.7 copy-start.6
  16.7 154.8 %all-gather.3.cloned.1.call-start = ((), (), s32[]{:S(2)}) async-start(), calls=%async_computation.9 | async-start | bytes 14155776 | tf_op jit(solution)/shard_map/all_gather | solution.py:34
  19.3 105.1 %copy-start.10 = (bf16[512,256]{1,0:T(8,128)(2,1)S(1)}, bf16[512,256]{1,0:T(8,128)(2,1)}, u32[]{:S(2)}) copy-start(bf16[512,256]{1,0:T(8,128)(2,1)} %param.12) | copy-start | bytes 786436
  19.3 241.9 %all-gather.5.cloned.1.call-start = ((), (), s32[]{:S(2)}) async-start(), calls=%async_computation.10 | async-start | bytes 1769472 | tf_op jit(solution)/shard_map/all_gather | solution.py:34
  20.3 151.2 %copy-start.11 = (f32[4096]{0:T(1024)S(1)}, f32[4096]{0:T(1024)}, u32[]{:S(2)}) copy-start(f32[4096]{0:T(1024)} %param.15) | copy-start | bytes 49156
  125.4 52.9 %copy-start.5 = (bf16[512,256]{1,0:T(8,128)(2,1)}, bf16[512,256]{1,0:T(8,128)(2,1)S(1)}, u32[]{:S(2)}) copy-start(bf16[512,256]{1,0:T(8,128)(2,1)S(1)} %add_convert_fusion) | copy-start | bytes 786436
  178.3 3.7 %copy-start.4 = (bf16[512,4096]{1,0:T(8,128)(2,1)S(1)}, bf16[512,4096]{1,0:T(8,128)(2,1)}, u32[]{:S(2)}) copy-start(bf16[512,4096]{1,0:T(8,128)(2,1)} %param.13) | copy-start | bytes 12582916
  223.2 39.5 %all-to-all-start.1 = ((bf16[64,8,512]{2,0,1:T(8,128)(2,1)}), bf16[64,8,512]{2,0,1:T(8,128)(2,1)S(1)}, u32[]{:S(2)}, u32[]{:S(2)}) async-start(bf16[64,8,512]{2,0,1:T(8,128)(2,1)} %fusion.13), calls=%async_computation.2 | async-start | bytes 1048576 | tf_op jit(solution)/shard_map/all_to_all | solution.py:140
  262.7 12.3 %all-to-all-start.6 = ((bf16[64,8,512]{2,0,1:T(8,128)(2,1)}), bf16[64,8,512]{2,0,1:T(8,128)(2,1)S(1)}, u32[]{:S(2)}, u32[]{:S(2)}) async-start(bf16[64,8,512]{2,0,1:T(8,128)(2,1)} %fusion.11), calls=%async_computation.7 | async-start | bytes 1048576 | tf_op jit(solution)/shard_map/all_to_all | solution.py:141
  275.0 2.9 %copy-start.2 = (bf16[8,512,512]{2,1,0:T(8,128)(2,1)S(1)}, bf16[8,512,512]{2,1,0:T(8,128)(2,1)}, u32[]{:S(2)}) copy-start(bf16[8,512,512]{2,1,0:T(8,128)(2,1)} %convolution_convert_fusion.2) | copy-start | bytes 12582916
  275.0 3.8 %copy-start.3 = (bf16[8,512,512]{2,1,0:T(8,128)(2,1)S(1)}, bf16[8,512,512]{2,1,0:T(8,128)(2,1)}, u32[]{:S(2)}) copy-start(bf16[8,512,512]{2,1,0:T(8,128)(2,1)} %convolution_convert_fusion.3) | copy-start | bytes 12582916
  276.3 5.0 %copy-start.1 = (bf16[256,512]{1,0:T(8,128)(2,1)S(1)}, bf16[256,512]{1,0:T(8,128)(2,1)}, u32[]{:S(2)}) copy-start(bf16[256,512]{1,0:T(8,128)(2,1)} %param.10) | copy-start | bytes 786436
Sparse Core Ops, SparseCore 0:
  16.8 107.5 reduce-scatter.1
Sparse Core Ops, SparseCore 1:
  19.4 152.1 all-gather.2
  220.9 40.3 all-gather.4
where the time goes:
time: 289 us
  waiting for transfers between devices  168 us (58%)
  blocking collectives  46.9 us (16%)
  matrix products  30 us (10%)
  between operations  15.8 us (5%)
  other arithmetic  11.1 us (4%)
  local copies, waits for them, and re-layouts  9.04 us (3%)
  starting transfers between devices  7.83 us (3%)
    reduce_scatter x1, waiting for transfers between devices, on_device(): lax.psum_scatter(lax.dot_general(out_weight, attn_values, (((0,), (1,)),...  88.8 us
    all_gather x2, waiting for transfers between devices, side_by_side(): lax.all_gather(both, axis, axis=dim, tiled=True)  77.5 us
    all_to_all x3, blocking collectives, from_everyone(): return lax.all_to_all(copies, axis, split_axis=0, concat_axis=0, tiled=True)  30.2 us
    all_to_all x1, blocking collectives, summed_rows(): lax.all_to_all(own.astype(jnp.bfloat16), far, 0, 0, tiled=True)  12.5 us
    dot_general x3, matrix products, grouped_product(): lax.dot_general(left, right, dims, preferred_element_type=jnp.float32)  7.81 us
    dot_general x1, matrix products, on_device(): lax.dot_general(out_weight, attn_values, (((0,), (1,)), ((), ())), prefer...  7.72 us
  transfers between devices with their start and end apart: 5, of which 4 were waited for; matrix products, arithmetic and copies ran while one was open for 6% of the time, Pallas kernels for 0%

commit v1 on v0

--- a/solution.py
+++ b/solution.py
@@ -7,6 +7,15 @@
 
 TENSOR = ("tensor_0", "tensor_1", "tensor_2")
 epsilon = 1e-05
+
+
+def run_numbers(tile_in, peer_axis):
+    return jnp.concatenate(
+        lax.all_to_all(
+            jnp.stack(jnp.split(tile_in, lax.psum(1, peer_axis), axis=1), axis=0), peer_axis, 0, 0
+        ),
+        axis=0,
+    )
 
 
 def from_everyone(value, axis):
@@ -138,7 +147,7 @@
     rows_local = w_gate.shape[0]
     every_normed, every_grad = (
         lax.all_to_all(normed, "batch", split_axis=1, concat_axis=0, tiled=True),
-        lax.all_to_all(grad_out, "batch", split_axis=1, concat_axis=0, tiled=True),
+        run_numbers(grad_out, "batch"),
     )
     every_gate, every_up, every_hidden = side_by_side(
         (grad_gate_act, grad_up_act, hidden), "batch", 0, 1

time: 289 us -> 290 us (level)
  local copies, waits for them, and re-layouts: 9.04 us -> 13.4 us
  waiting for transfers between devices: 168 us -> 165 us
    unnamed x26 -> x39, local copies, waits for them, and re-layouts: 3.15 us -> 7.6 us
  transfers between devices with their start and end apart: 5 -> 5, of which waited for: 4 -> 4; matrix products, arithmetic and copies ran while one was open for 6% -> 7% of each run, Pallas kernels for 0% -> 0%
where the time goes in v1:
time: 290 us; the launch traced here: 289 us
  waiting for transfers between devices  165 us (57%)
  blocking collectives  47 us (16%)
  matrix products  30 us (10%)
  between operations  15.8 us (5%)
  local copies, waits for them, and re-layouts  13.4 us (5%)
  other arithmetic  9.85 us (3%)
  starting transfers between devices  7.65 us (3%)
    reduce_scatter x1, waiting for transfers between devices, on_device(): lax.psum_scatter(lax.dot_general(out_weight, attn_values, (((0,), (1,)),...  88.8 us
    all_gather x2, waiting for transfers between devices, side_by_side(): lax.all_gather(both, axis, axis=dim, tiled=True)  74.7 us
    all_to_all x3, blocking collectives, from_everyone(): return lax.all_to_all(copies, axis, split_axis=0, concat_axis=0, tiled=True)  30.4 us
    all_to_all x1, blocking collectives, summed_rows(): lax.all_to_all(own.astype(jnp.bfloat16), far, 0, 0, tiled=True)  12.5 us
    dot_general x3, matrix products, grouped_product(): lax.dot_general(left, right, dims, preferred_element_type=jnp.float32)  7.8 us
    dot_general x1, matrix products, on_device(): lax.dot_general(out_weight, attn_values, (((0,), (1,)), ((), ())), prefer...  7.72 us
    unnamed x39, local copies, waits for them, and re-layouts  7.6 us
  transfers between devices with their start and end apart: 5, of which 4 were waited for; matrix products, arithmetic and copies ran while one was open for 7% of the time, Pallas kernels for 0%

profile of v1, /device:TPU:18, one launch (start us, length us, event | category | flops | bytes accessed | tf_op | source)
XLA Modules:
  0.0 289.1 jit_solution(9378865586707072909)
XLA Ops:
  8.1 0.9 copy-done
  9.0 7.7 %convolution_convert_fusion = bf16[8192,256]{1,0:T(8,128)(2,1)} fusion(bf16[512,8192]{1,0:T(8,128)(2,1)} %param.11, bf16[256,512]{1,0:T(8,128)(2,1)S(1)} %copy-done), kind=kOutput, calls=%fused_computation.2 | convolution fusion | flops 2149580800 | bytes 12845056 | tf_op jit(solution)/shard_map/dot_general | solution.py:104
  16.8 0.9 copy-done.7
  18.0 1.3 pad_maximum_fusion
  19.4 0.7 gather_fusion
  20.3 14.8 %all_to_all.43 = bf16[16,64,256]{2,1,0:T(8,128)(2,1)S(1)} all-to-all(bf16[16,64,256]{2,1,0:T(8,128)(2,1)S(1)} %broadcast_in_dim.74), channel_id=1, replica_groups=mesh['batch'=8,'tensor_0'=2,'tensor_1'=4,'tensor_2'=2] {'tensor_0','tens..., dimensions={0} | all-to-all | bytes 1048576 | tf_op jit(solution)/shard_map/all_to_all | solution.py:23
  35.6 88.8 %reduce-scatter.2.cloned.1.call-done = bf16[512,256]{1,0:T(8,128)(2,1)} async-done(((bf16[8192,256]{1,0:T(8,128)(2,1)}), bf16[512,256]{1,0:T(8,128)(2,1)}) %reduce-scatter.2.cloned.1.call-update) | async-done | bytes 262160 | tf_op jit(solution)/shard_map/reduce_scatter | solution.py:103
  124.4 1.0 add_convert_fusion
  125.6 0.7 gather_fusion.1
  126.3 45.2 %all-gather.3.cloned.1.call-done = bf16[4096,1536]{1,0:T(8,128)(2,1)} async-done(((bf16[512,1536]{1,0:T(8,128)(2,1)}), bf16[4096,1536]{1,0:T(8,128)(2,1)}) %all-gather.3.cloned.1.call-update) | async-done | bytes 12582928 | tf_op jit(solution)/shard_map/all_gather | solution.py:43
  171.5 3.1 %fusion.3 = f32[64,512]{1,0:T(8,128)S(1)} fusion(bf16[4096,1536]{1,0:T(8,128)(2,1)} %all-gather.3.cloned.1.call-done, f32[64,4096]{1,0:T(8,128)S(1)} %bitcast.69, f32[4096]{0:T(1024)S(1)} %copy-done.11, f32[64]{0:T(128)S(1)} %add_rsqrt_fusion), kind=kOutput, calls=%fused_computation.10 | convolution fusion | flops 269221888 | bytes 5390592 | tf_op jit(solution)/shard_map/dot_general | solution.py:128
  174.6 3.8 %multiply_convert_fusion.4 = (bf16[64,512]{1,0:T(8,128)(2,1)S(1)}, f32[64,512]{1,0:T(8,128)}) fusion(f32[64,512]{1,0:T(8,128)S(1)} %fusion.3, bf16[4096,1536]{1,0:T(8,128)(2,1)} %all-gather.3.cloned.1.call-done, f32[64,4096]{1,0:T(8,128)S(1)} %bitcast.70, f32[4096]{0:T(1024)S(1)} %copy-done.11, f32[64]{0:T(128)S(1)} %add_rsqrt_fusion), kind=kOutput, calls=%fused_computation.37 | convolution fusion | flops 269418496 | bytes 5587200 | tf_op jit(solution)/shard_map/dot_general | solution.py:129
  178.4 3.7 %fusion.7 = f32[64,4096]{1,0:T(8,128)S(1)} fusion(bf16[64,512]{1,0:T(8,128)(2,1)S(1)} %get-tuple-element.13, bf16[4096,1536]{1,0:T(8,128)(2,1)} %all-gather.3.cloned.1.call-done), kind=kOutput, calls=%fused_computation.14 | convolution fusion | flops 268435456 | bytes 5308416 | tf_op jit(solution)/shard_map/dot_general | solution.py:132
  182.1 0.9 fusion
  183.4 4.2 %all_to_all.44 = bf16[2,8,4,4096]{3,2,1,0:T(4,128)(2,1)S(1)} all-to-all(bf16[2,8,4,4096]{3,2,1,0:T(4,128)(2,1)S(1)} %bitcast.68), channel_id=1, replica_groups=mesh['batch'=8,'tensor_0'=2,'tensor_1'=4,'tensor_2'=2] {'tensor_2'}, dimensions={0} | all-to-all | bytes 1048576 | tf_op jit(solution)/shard_map/all_to_all | solution.py:54
  188.1 12.5 %all_to_all.45 = bf16[8,4,4096]{2,1,0:T(4,128)(2,1)S(1)} all-to-all(bf16[8,4,4096]{2,1,0:T(4,128)(2,1)S(1)} %reduce_sum.61), channel_id=1, replica_groups=mesh['batch'=8,'tensor_0'=2,'tensor_1'=4,'tensor_2'=2] {'tensor_0','tens..., dimensions={0} | all-to-all | bytes 524288 | tf_op jit(solution)/shard_map/all_to_all | solution.py:62
  200.8 11.3 %all_to_all.46 = bf16[8,4,4096]{2,1,0:T(4,128)(2,1)S(1)} all-to-all(bf16[8,4,4096]{2,1,0:T(4,128)(2,1)S(1)} %broadcast_in_dim.80), channel_id=1, replica_groups=mesh['batch'=8,'tensor_0'=2,'tensor_1'=4,'tensor_2'=2] {'tensor_0','tens..., dimensions={0} | all-to-all | bytes 524288 | tf_op jit(solution)/shard_map/all_to_all | solution.py:23
  212.4 4.3 %all_to_all.47 = bf16[2,8,4,4096]{3,2,1,0:T(4,128)(2,1)S(1)} all-to-all(bf16[2,8,4,4096]{3,2,1,0:T(4,128)(2,1)S(1)} %broadcast_in_dim.81), channel_id=1, replica_groups=mesh['batch'=8,'tensor_0'=2,'tensor_1'=4,'tensor_2'=2] {'tensor_2'}, dimensions={0} | all-to-all | bytes 1048576 | tf_op jit(solution)/shard_map/all_to_all | solution.py:23
  217.4 3.0 %multiply_convert_fusion.3 = (bf16[64,512]{1,0:T(8,128)(2,1)S(1)}, bf16[64,512]{1,0:T(8,128)(2,1)S(1)}) fusion(f32[64,512]{1,0:T(8,128)S(1)} %copy-done.14, f32[64,512]{1,0:T(8,128)S(1)} %copy-done.15, bf16[64,4096]{1,0:T(8,128)(2,1)S(1)} %multiply_convert_fusion, bf16[4096,1536]{1,0:T(8,128)(2,1)} %all-gather.3.cloned.1.call-done), kind=kOutput, calls=%fused_computation.36 | convolution fusion | flops 268861440 | bytes 5111808 | tf_op jit(solution)/shard_map/dot_general | solution.py:142
  220.5 0.7 pad_maximum_fusion.1
  222.1 1.4 fusion.11
  223.5 3.5 %all-to-all-start.1 = ((bf16[64,8,512]{2,0,1:T(8,128)(2,1)}), bf16[64,8,512]{2,0,1:T(8,128)(2,1)S(1)}, u32[]{:S(2)}, u32[]{:S(2)}) async-start(bf16[64,8,512]{2,0,1:T(8,128)(2,1)} %fusion.11), calls=%async_computation.2 | async-start | bytes 1048576 | tf_op jit(solution)/shard_map/all_to_all | solution.py:149
  232.1 29.5 %all-gather.5.cloned.1.call-done = bf16[512,1536]{1,0:T(8,128)(2,1)} async-done(((bf16[64,1536]{1,0:T(8,128)(2,1)}), bf16[512,1536]{1,0:T(8,128)(2,1)}) %all-gather.5.cloned.1.call-update) | async-done | bytes 1572880 | tf_op jit(solution)/shard_map/all_gather | solution.py:43
  261.6 1.5 fusion.30
  263.1 4.0 %all-to-all-start.6 = ((bf16[8,64,512]{2,1,0:T(8,128)(2,1)}), bf16[8,64,512]{2,1,0:T(8,128)(2,1)S(1)}, u32[]{:S(2)}, u32[]{:S(2)}) async-start(bf16[8,64,512]{2,1,0:T(8,128)(2,1)} %fusion.14), calls=%async_computation.7 | async-start | bytes 1048576 | tf_op jit(solution)/shard_map/all_to_all | solution.py:14
  267.1 3.2 %convolution_convert_fusion.2 = bf16[8,512,512]{2,1,0:T(8,128)(2,1)} fusion(bf16[8,64,512]{2,1,0:T(8,128)(2,1)S(1)} %bitcast.67, bf16[64,8,512]{2,0,1:T(8,128)(2,1)S(1)} %all-to-all-done.1), kind=kOutput, calls=%fused_computation.17 | convolution fusion | flops 270532608 | bytes 5242880 | tf_op jit(solution)/shard_map/dot_general | solution.py:86
  270.3 3.3 %convolution_convert_fusion.3 = bf16[8,512,512]{2,1,0:T(8,128)(2,1)} fusion(bf16[8,64,512]{2,1,0:T(8,128)(2,1)S(1)} %bitcast.66, bf16[64,8,512]{2,0,1:T(8,128)(2,1)S(1)} %all-to-all-done.1), kind=kOutput, calls=%fused_computation.18 | convolution fusion | flops 270532608 | bytes 5242880 | tf_op jit(solution)/shard_map/dot_general | solution.py:86
  273.6 1.8 all-to-all-done.6
  275.4 1.3 convolution_convert_fusion.1
  276.7 1.6 convert_reduce_fusion
  278.3 0.9 copy-done.3
  279.2 2.5 convert_reduce_fusion.1
  (67 shorter events, 9.4 us)
Async XLA Ops:
  8.0 1.0 copy-start
  8.0 116.4 %reduce-scatter.2.cloned.1.call-start = ((), (), s32[]{:S(2)}) async-start(), calls=%async_computation.8 | async-start | bytes 4456448 | tf_op jit(solution)/shard_map/reduce_scatter | solution.py:103
  16.7 1.0 copy-start.7
  16.7 1.2 copy-start.8
  16.7 1.4 copy-start.9
  16.7 2.7 copy-start.12
  16.7 2.7 copy-start.6
  16.7 154.8 %all-gather.3.cloned.1.call-start = ((), (), s32[]{:S(2)}) async-start(), calls=%async_computation.9 | async-start | bytes 14155776 | tf_op jit(solution)/shard_map/all_gather | solution.py:43
  19.3 105.1 %copy-start.10 = (bf16[512,256]{1,0:T(8,128)(2,1)S(1)}, bf16[512,256]{1,0:T(8,128)(2,1)}, u32[]{:S(2)}) copy-start(bf16[512,256]{1,0:T(8,128)(2,1)} %param.12) | copy-start | bytes 786436
  19.3 242.3 %all-gather.5.cloned.1.call-start = ((), (), s32[]{:S(2)}) async-start(), calls=%async_computation.10 | async-start | bytes 1769472 | tf_op jit(solution)/shard_map/all_gather | solution.py:43
  20.3 151.2 %copy-start.11 = (f32[4096]{0:T(1024)S(1)}, f32[4096]{0:T(1024)}, u32[]{:S(2)}) copy-start(f32[4096]{0:T(1024)} %param.15) | copy-start | bytes 49156
  125.4 53.0 %copy-start.5 = (bf16[512,256]{1,0:T(8,128)(2,1)}, bf16[512,256]{1,0:T(8,128)(2,1)S(1)}, u32[]{:S(2)}) copy-start(bf16[512,256]{1,0:T(8,128)(2,1)S(1)} %add_convert_fusion) | copy-start | bytes 786436
  174.6 7.5 %copy-start.13 = (f32[64,512]{1,0:T(8,128)}, f32[64,512]{1,0:T(8,128)S(1)}, u32[]{:S(2)}) copy-start(f32[64,512]{1,0:T(8,128)S(1)} %fusion.3) | copy-start | bytes 393220
  178.4 3.7 %copy-start.4 = (bf16[512,4096]{1,0:T(8,128)(2,1)S(1)}, bf16[512,4096]{1,0:T(8,128)(2,1)}, u32[]{:S(2)}) copy-start(bf16[512,4096]{1,0:T(8,128)(2,1)} %param.13) | copy-start | bytes 12582916
  212.4 5.1 %copy-start.14 = (f32[64,512]{1,0:T(8,128)S(1)}, f32[64,512]{1,0:T(8,128)}, u32[]{:S(2)}) copy-start(f32[64,512]{1,0:T(8,128)} %copy-done.13) | copy-start | bytes 393220
  212.4 5.0 %copy-start.15 = (f32[64,512]{1,0:T(8,128)S(1)}, f32[64,512]{1,0:T(8,128)}, u32[]{:S(2)}) copy-start(f32[64,512]{1,0:T(8,128)} %get-tuple-element.14) | copy-start | bytes 393220
  223.5 39.5 %all-to-all-start.1 = ((bf16[64,8,512]{2,0,1:T(8,128)(2,1)}), bf16[64,8,512]{2,0,1:T(8,128)(2,1)S(1)}, u32[]{:S(2)}, u32[]{:S(2)}) async-start(bf16[64,8,512]{2,0,1:T(8,128)(2,1)} %fusion.11), calls=%async_computation.2 | async-start | bytes 1048576 | tf_op jit(solution)/shard_map/all_to_all | solution.py:149
  263.1 12.3 %all-to-all-start.6 = ((bf16[8,64,512]{2,1,0:T(8,128)(2,1)}), bf16[8,64,512]{2,1,0:T(8,128)(2,1)S(1)}, u32[]{:S(2)}, u32[]{:S(2)}) async-start(bf16[8,64,512]{2,1,0:T(8,128)(2,1)} %fusion.14), calls=%async_computation.7 | async-start | bytes 1048576 | tf_op jit(solution)/shard_map/all_to_all | solution.py:14
  275.4 2.9 %copy-start.2 = (bf16[8,512,512]{2,1,0:T(8,128)(2,1)S(1)}, bf16[8,512,512]{2,1,0:T(8,128)(2,1)}, u32[]{:S(2)}) copy-start(bf16[8,512,512]{2,1,0:T(8,128)(2,1)} %convolution_convert_fusion.2) | copy-start | bytes 12582916
  275.4 3.8 %copy-start.3 = (bf16[8,512,512]{2,1,0:T(8,128)(2,1)S(1)}, bf16[8,512,512]{2,1,0:T(8,128)(2,1)}, u32[]{:S(2)}) copy-start(bf16[8,512,512]{2,1,0:T(8,128)(2,1)} %convolution_convert_fusion.3) | copy-start | bytes 12582916
  276.7 5.0 %copy-start.1 = (bf16[256,512]{1,0:T(8,128)(2,1)S(1)}, bf16[256,512]{1,0:T(8,128)(2,1)}, u32[]{:S(2)}) copy-start(bf16[256,512]{1,0:T(8,128)(2,1)} %param.10) | copy-start | bytes 786436
Sparse Core Ops, SparseCore 0:
  16.8 107.5 reduce-scatter.1
Sparse Core Ops, SparseCore 1:
  19.4 152.1 all-gather.2
  221.3 40.3 all-gather.4
